TPU v7x, 256 devices: a whole 4x4x8 slice. The times are simulated.
256 devices in a mesh: ctx: 64 (over y, z, core), head: 4 (over x).
Axes of the slice: x: 4, y: 4, z: 8, core: 2. Of those that a mesh axis runs over, the one named last changes fastest.
Arguments:
- query: bfloat16 [8192, 32, 128], P('ctx', 'head'), may hold values from -6 to 6
- key: bfloat16 [8192, 4, 128], P(('ctx', 'head')), may hold values from -6 to 6
- value: bfloat16 [8192, 4, 128], P(('ctx', 'head')), may hold values from -6 to 6
- d_out: bfloat16 [8192, 32, 128], P('ctx', 'head'), may hold values from -6 to 6
- seg_blocks: int32 [32], replicated, may hold values from 1 to 4, 64 in all
- seg_audio: int32 [32], replicated, may hold values 0 or 1
Outputs:
- d_query: bfloat16 [8192, 32, 128], P('ctx', 'head')
- d_key: bfloat16 [8192, 4, 128], P(('ctx', 'head'))
- d_value: bfloat16 [8192, 4, 128], P(('ctx', 'head'))
Inputs may be any that keep to these rules, and one draw needn't show every extreme that they name: `seg_blocks`: the segments tile the 64 blocks in order: their lengths sum to 64.
All inputs are finite; a program needn't handle non-finite values.
Results may differ from a plain program's by a relative error of at most 0.0055.
Values may be sent and summed in bfloat16 or wider, within the bound.
No kernel may reach another device: no remote copies, remote signals or barrier semaphores. Data moves between devices by JAX's collectives and lax.ppermute only.
A program may use at most 128 MiB of HBM per device.

v0:
```python
import math
import jax
import jax.numpy as jnp
from jax import lax
from jax.sharding import PartitionSpec as P

DH = 128
GROUP = 8
BLK = 128
NEG = -1e30


def segment_tables(seg_blocks, seg_audio, positions):
    ends = jnp.cumsum(seg_blocks)
    starts = ends - seg_blocks
    blocks = positions // BLK
    inside = (starts[None, :] <= blocks[:, None]) & (blocks[:, None] < ends[None, :])
    numbers = jnp.arange(seg_blocks.shape[0], dtype=jnp.int32)
    segment = jnp.sum(jnp.where(inside, numbers[None, :], 0), axis=1)
    audio = jnp.sum(jnp.where(inside, seg_audio[None, :], 0), axis=1)
    return (segment, audio)


def visible(query_pos, key_pos, query_seg, query_audio, key_seg):
    causal = key_pos[None, :] <= query_pos[:, None]
    span = (query_seg[:, None] == key_seg[None, :]) & (query_audio[:, None] == 1)
    return causal | span


def prepare(rows_query, rows_out, query_pos, seg_blocks, seg_audio):
    tokens = rows_query.shape[0]
    query_seg, query_audio = segment_tables(seg_blocks, seg_audio, query_pos)
    query_flat = rows_query.reshape(tokens * GROUP, DH)
    out_flat = rows_out.reshape(tokens * GROUP, DH)
    return (query_flat, out_flat, query_pos, query_seg, query_audio)


def piece_mask(group_data, keys, seg_blocks, seg_audio):
    query_flat, out_flat, query_pos, query_seg, query_audio = group_data
    key_pos = jnp.arange(keys.shape[0], dtype=jnp.int32)
    key_seg = segment_tables(seg_blocks, seg_audio, key_pos)[0]
    return visible(query_pos, key_pos, query_seg, query_audio, key_seg)


def contract_rows(left, right):
    return lax.dot_general(
        left, right, (((1,), (1,)), ((), ())), preferred_element_type=jnp.float32
    )


def contract_first(left, right):
    return lax.dot_general(
        left, right, (((0,), (0,)), ((), ())), preferred_element_type=jnp.float32
    )


def stats_group(group_data, state, piece, seg_blocks, seg_audio):
    query_flat, out_flat, query_pos, query_seg, query_audio = group_data
    keys, values = piece
    count = keys.shape[0]
    tokens = query_pos.shape[0]
    scale = 1.0 / math.sqrt(DH)
    mask = piece_mask(group_data, keys, seg_blocks, seg_audio)

    def stats_compute(kept):
        highest, total, weighted = kept
        wide = mask[:, None, :]
        scores = (contract_rows(query_flat, keys) * scale).reshape(tokens, GROUP, count)
        new_high = jnp.maximum(highest, jnp.max(jnp.where(wide, scores, NEG), axis=2))
        probs = jnp.where(wide, jnp.exp(scores - new_high[:, :, None]), 0.0)
        d_probs = contract_rows(out_flat, values).reshape(tokens, GROUP, count)
        return (new_high, jnp.sum(probs, axis=2), jnp.sum(probs * d_probs, axis=2))

    def stats_skipped(kept):
        return kept

    return lax.cond(jnp.any(mask), stats_compute, stats_skipped, state)


def grad_group(group_data, finals, grad_rows, piece, seg_blocks, seg_audio):
    query_flat, out_flat, query_pos, query_seg, query_audio = group_data
    lse, delta = finals
    keys, values = piece
    count = keys.shape[0]
    tokens = query_pos.shape[0]
    scale = 1.0 / math.sqrt(DH)
    mask = piece_mask(group_data, keys, seg_blocks, seg_audio)

    def grad_compute(grad_rows):
        wide = mask[:, None, :]
        scores = (contract_rows(query_flat, keys) * scale).reshape(tokens, GROUP, count)
        probs = jnp.where(wide, jnp.exp(scores - lse[:, :, None]), 0.0)
        d_probs = contract_rows(out_flat, values).reshape(tokens, GROUP, count)
        probs_low = probs.astype(jnp.bfloat16).reshape(tokens * GROUP, count)
        d_scores = (
            (probs * (d_probs - delta[:, :, None]))
            .astype(jnp.bfloat16)
            .reshape(tokens * GROUP, count)
        )
        value_part = contract_first(probs_low, out_flat)
        key_part = contract_first(d_scores, query_flat)
        grad_rows = jnp.dot(d_scores, keys, preferred_element_type=jnp.float32)
        return (grad_rows, key_part, value_part)

    def grad_skipped(grad_rows):
        blank = jnp.zeros((count, keys.shape[1]), jnp.float32)
        return (grad_rows, blank, blank)

    return lax.cond(jnp.any(mask), grad_compute, grad_skipped, grad_rows)


def body(query, key, value, d_out, seg_blocks, seg_audio):
    key, value = (
        lax.all_to_all(key, "head", split_axis=1, concat_axis=0, tiled=True),
        lax.all_to_all(value, "head", split_axis=1, concat_axis=0, tiled=True),
    )
    rows = query.shape[0]
    half = rows // 2
    place = lax.axis_index("ctx")
    scale = 1.0 / math.sqrt(DH)
    keys = key[:, 0, :]
    values = value[:, 0, :]
    own_pos = place * rows + jnp.arange(rows, dtype=jnp.int32)
    first = prepare(query[:half], d_out[:half], own_pos[:half], seg_blocks, seg_audio)
    second = prepare(query[half:], d_out[half:], own_pos[half:], seg_blocks, seg_audio)
    groups = (first, second)
    blank_stats = jnp.zeros((half, GROUP), jnp.float32)
    start_stats = tuple(
        (
            (jnp.full((half, GROUP), NEG, jnp.float32), blank_stats, blank_stats)
            for group_data in groups
        )
    )
    piece = (
        lax.all_gather(keys, "ctx", axis=0, tiled=True),
        lax.all_gather(values, "ctx", axis=0, tiled=True),
    )
    stats = tuple(
        (
            stats_group(group_data, state, piece, seg_blocks, seg_audio)
            for group_data, state in zip(groups, start_stats)
        )
    )
    finals = tuple(
        ((highest + jnp.log(total), weighted / total) for highest, total, weighted in stats)
    )
    blank_rows = jnp.zeros((half * GROUP, DH), jnp.float32)
    piece = (
        lax.all_gather(keys, "ctx", axis=0, tiled=True),
        lax.all_gather(values, "ctx", axis=0, tiled=True),
    )
    grad_list = (blank_rows, blank_rows)
    piece_keys = piece[0]
    count = piece_keys.shape[0]
    key_sum = jnp.zeros((count, DH), jnp.float32)
    value_sum = jnp.zeros((count, DH), jnp.float32)
    new_rows = []
    for group_data, group_finals, grad_rows in zip(groups, finals, grad_list):
        grad_rows, key_part, value_part = grad_group(
            group_data, group_finals, grad_rows, piece, seg_blocks, seg_audio
        )
        key_sum = key_sum + key_part
        value_sum = value_sum + value_part
        new_rows.append(grad_rows)
    update = jnp.stack([key_sum, value_sum], axis=1)
    key_grad = update
    grads = (key_grad, tuple(new_rows))
    key_grad, grad_list = grads
    summed = lax.psum_scatter(key_grad, "ctx", scatter_dimension=0, tiled=True)
    d_key = (summed[:, 0, :] * scale).astype(jnp.bfloat16)[:, None, :]
    d_value = summed[:, 1, :].astype(jnp.bfloat16)[:, None, :]
    first_rows = (grad_list[0] * scale).astype(jnp.bfloat16).reshape(half, GROUP, DH)
    second_rows = (grad_list[1] * scale).astype(jnp.bfloat16).reshape(half, GROUP, DH)
    d_query = jnp.concatenate([first_rows, second_rows], axis=0)
    d_key, d_value = (
        lax.all_to_all(d_key, "head", split_axis=0, concat_axis=1, tiled=True),
        lax.all_to_all(d_value, "head", split_axis=0, concat_axis=1, tiled=True),
    )
    return (d_query, d_key, d_value)


def solution(mesh):
    placed = (
        P("ctx", "head", None),
        P(("ctx", "head"), None, None),
        P(("ctx", "head"), None, None),
        P("ctx", "head", None),
        P(),
        P(),
    )
    return jax.shard_map(
        body,
        mesh=mesh,
        in_specs=placed,
        out_specs=(
            P("ctx", "head", None),
            P(("ctx", "head"), None, None),
            P(("ctx", "head"), None, None),
        ),
        check_vma=False,
    )
```

profile of v0, /device:TPU:8, one launch (start us, length us, event | category | flops | bytes accessed | tf_op | source)
XLA Modules:
  0.0 555.6 jit_solution(9331188242737443876)
XLA Ops:
  8.0 9.6 %all_to_all.66 = bf16[32,4,128]{2,0,1:T(8,128)(2,1)} all-to-all(bf16[32,4,128]{2,0,1:T(8,128)(2,1)S(1)} %copy.34), channel_id=1, replica_groups=mesh['ctx'=64,'head'=4] {'head'}, dimensions={1} | all-to-all | bytes 65536 | tf_op jit(solution)/shard_map/all_to_all | solution.py:114
  18.5 8.5 %all_to_all.67 = bf16[32,4,128]{2,0,1:T(8,128)(2,1)} all-to-all(bf16[32,4,128]{2,0,1:T(8,128)(2,1)S(1)} %copy.35), channel_id=1, replica_groups=mesh['ctx'=64,'head'=4] {'head'}, dimensions={1} | all-to-all | bytes 65536 | tf_op jit(solution)/shard_map/all_to_all | solution.py:115
  35.2 60.1 %all-gather.3.cloned.1.call-done = bf16[8192,128]{1,0:T(8,128)(2,1)} async-done(((bf16[128,128]{1,0:T(8,128)(2,1)}), bf16[8192,128]{1,0:T(8,128)(2,1)}) %all-gather.3.cloned.1.call-update) | async-done | bytes 2097168 | tf_op jit(solution)/shard_map/all_gather | solution.py:149
  95.2 77.8 %all-gather.5.cloned.1.call-done = bf16[8192,128]{1,0:T(8,128)(2,1)} async-done(((bf16[128,128]{1,0:T(8,128)(2,1)}), bf16[8192,128]{1,0:T(8,128)(2,1)}) %all-gather.5.cloned.1.call-update) | async-done | bytes 2097168 | tf_op jit(solution)/shard_map/all_gather | solution.py:136
  173.0 30.0 %conditional.4 = (f32[64,8]{1,0:T(8,128)}, f32[64,8]{1,0:T(8,128)}, f32[64,8]{1,0:T(8,128)}) conditional(s32[]{:T(128)} %convert_element_type.36, () %tuple.57, (pred[64,8192]{1,0:T(8,128)(4,1)S(1)}, bf16[512,128]{1,0:T(8,128)(2,1)S(1)}, bf16[8192,128]{1,0:T(8,128)(2,1)}, bf16[512,128]{1,0:T(8,128)(2,1)}, bf16[8192,128]{1,0:T(8,128)(2,1)}) %tuple.58), branch_computations={%region_5.6_spmd, %region_6.10_spmd} | conditional | flops 2197814784 | bytes 65308752 | solution.py:77
  173.0 9.5 %fusion = (f32[512]{0:T(512)S(1)}, f32[512,8192]{1,0:T(8,128)}) fusion(pred[64,8192]{1,0:T(8,128)(4,1)S(1)} %get-tuple-element.80, bf16[512,128]{1,0:T(8,128)(2,1)S(1)} %get-tuple-element.81, bf16[8192,128]{1,0:T(8,128)(2,1)} %get-tuple-element.82), kind=kOutput, calls=%fused_computation.2 | convolution fusion | flops 1086324224 | bytes 19531776 | tf_op jit(solution)/shard_map/cond/branch_1_fun/dot_general | solution.py:46
  182.6 9.9 %multiply_reduce_fusion = f32[512]{0:T(512)S(1)} fusion(bf16[512,128]{1,0:T(8,128)(2,1)S(1)} %copy-done.10, bf16[8192,128]{1,0:T(8,128)(2,1)S(1)} %copy-done.6, f32[512,8192]{1,0:T(8,128)} %get-tuple-element.172, f32[512]{0:T(512)S(1)} %broadcast_maximum_fusion, pred[64,8192]{1,0:T(8,128)(4,1)S(1)} %get-tuple-element.80), kind=kOutput, calls=%fused_computation.3 | convolution fusion | flops 1094712832 | bytes 19533824 | tf_op jit(solution)/shard_map/cond/branch_1_fun/dot_general | solution.py:46
  192.5 8.5 %fusion.1 = f32[512]{0:T(512)S(1)} fusion(f32[512,8192]{1,0:T(8,128)} %get-tuple-element.172, f32[512]{0:T(512)S(1)} %broadcast_maximum_fusion, pred[64,8192]{1,0:T(8,128)(4,1)S(1)} %get-tuple-element.80), kind=kLoop, calls=%fused_computation.4 | loop fusion | flops 16776704 | bytes 17305600 | tf_op jit(solution)/shard_map/cond/branch_1_fun/reduce_sum | solution.py:72
  203.1 38.1 %conditional.5 = (f32[512,128]{1,0:T(8,128)S(1)}, f32[8192,128]{1,0:T(8,128)}, f32[8192,128]{1,0:T(8,128)}) conditional(s32[]{:T(128)} %convert_element_type.36, () %tuple.56, (pred[64,8192]{1,0:T(8,128)(4,1)S(1)}, bf16[512,128]{1,0:T(8,128)(2,1)S(1)}, bf16[8192,128]{1,0:T(8,128)(2,1)}, f32[64,8]{1,0:T(8,128)}, f32[64,8]{1,0:T(8,128)}, ...), branch_computations={%region_10.11_spmd, %region_11.12_spmd} | conditional | flops 5398069760 | bytes 209471680 | solution.py:109
  205.3 6.2 %exponential_select_fusion = f32[512,8192]{1,0:T(8,128)S(1)} fusion(bf16[512,128]{1,0:T(8,128)(2,1)S(1)} %get-tuple-element.86, bf16[8192,128]{1,0:T(8,128)(2,1)} %get-tuple-element.87, f32[512]{0:T(512)S(1)} %sub.81, pred[64,8192]{1,0:T(8,128)(4,1)S(1)} %get-tuple-element.85), kind=kOutput, calls=%fused_computation.7 | convolution fusion | flops 1086324736 | bytes 19531776 | tf_op jit(solution)/shard_map/cond/branch_1_fun/dot_general | solution.py:46
  211.5 5.7 %copy-done = f32[512,8192]{1,0:T(8,128)} copy-done((f32[512,8192]{1,0:T(8,128)}, f32[512,8192]{1,0:T(8,128)S(1)}, u32[]{:S(2)}) %copy-start) | copy-done | bytes 16777240 | tf_op jit(solution)/shard_map/cond
  221.6 9.4 %multiply_convert_fusion = bf16[512,8192]{1,0:T(8,128)(2,1)} fusion(f32[512,8192]{1,0:T(8,128)} %copy-done, bf16[512,128]{1,0:T(8,128)(2,1)S(1)} %copy-done.11, bf16[8192,128]{1,0:T(8,128)(2,1)S(1)} %copy-done.7, f32[512]{0:T(512)S(1)} %sub.84), kind=kOutput, calls=%fused_computation.6 | convolution fusion | flops 1086324736 | bytes 27396096 | tf_op jit(solution)/shard_map/cond/branch_1_fun/dot_general | solution.py:46
  231.0 5.9 %fusion.23 = f32[512,128]{1,0:T(8,128)S(1)} fusion(bf16[512,8192]{1,0:T(8,128)(2,1)} %multiply_convert_fusion, bf16[8192,128]{1,0:T(8,128)(2,1)S(1)} %copy-done.4), kind=kOutput, calls=%fused_computation.67 | convolution fusion | flops 1073741824 | bytes 10747904 | tf_op jit(solution)/shard_map/cond/branch_1_fun/dot_general | solution.py:102
  241.2 28.4 %conditional.6 = (f32[64,8]{1,0:T(8,128)S(1)}, f32[64,8]{1,0:T(8,128)S(1)}, f32[64,8]{1,0:T(8,128)S(1)}) conditional(s32[]{:T(128)} %convert_element_type.38, () %tuple.61, (pred[64,8192]{1,0:T(8,128)(4,1)S(1)}, bf16[512,128]{1,0:T(8,128)(2,1)S(1)}, bf16[8192,128]{1,0:T(8,128)(2,1)}, bf16[512,128]{1,0:T(8,128)(2,1)S(1)}, ...), branch_computations={%region_15.16_spmd, %region_16.20_spmd} | conditional | flops 2197814784 | bytes 64784436 | solution.py:77
  241.4 9.6 %fusion.4 = (f32[512]{0:T(512)S(1)}, f32[512,8192]{1,0:T(8,128)}) fusion(pred[64,8192]{1,0:T(8,128)(4,1)S(1)} %get-tuple-element.93, bf16[512,128]{1,0:T(8,128)(2,1)S(1)} %get-tuple-element.94, bf16[8192,128]{1,0:T(8,128)(2,1)} %get-tuple-element.95), kind=kOutput, calls=%fused_computation.12 | convolution fusion | flops 1086324224 | bytes 19531776 | tf_op jit(solution)/shard_map/cond/branch_1_fun/dot_general | solution.py:46
  250.9 9.9 %multiply_reduce_fusion.1 = f32[512]{0:T(512)S(1)} fusion(bf16[512,128]{1,0:T(8,128)(2,1)S(1)} %get-tuple-element.96, bf16[8192,128]{1,0:T(8,128)(2,1)S(1)} %copy-done.8, f32[512,8192]{1,0:T(8,128)} %get-tuple-element.176, f32[512]{0:T(512)S(1)} %broadcast_maximum_fusion.1, pred[64,8192]{1,0:T(8,128)(4,1)S(1)} %get-tuple-element.93), kind=kOutput, calls=%fused_computation.13 | convolution fusion | flops 1094712832 | bytes 19533824 | tf_op jit(solution)/shard_map/cond/branch_1_fun/dot_general | solution.py:46
  260.8 8.5 %fusion.5 = f32[512]{0:T(512)S(1)} fusion(f32[512,8192]{1,0:T(8,128)} %get-tuple-element.176, f32[512]{0:T(512)S(1)} %broadcast_maximum_fusion.1, pred[64,8192]{1,0:T(8,128)(4,1)S(1)} %get-tuple-element.93), kind=kLoop, calls=%fused_computation.14 | loop fusion | flops 16776704 | bytes 17305600 | tf_op jit(solution)/shard_map/cond/branch_1_fun/reduce_sum | solution.py:72
  269.6 36.6 %conditional.7 = (f32[512,128]{1,0:T(8,128)S(1)}, f32[8192,128]{1,0:T(8,128)}, f32[8192,128]{1,0:T(8,128)}) conditional(s32[]{:T(128)} %convert_element_type.38, () %tuple.60, (pred[64,8192]{1,0:T(8,128)(4,1)S(1)}, bf16[512,128]{1,0:T(8,128)(2,1)S(1)}, bf16[8192,128]{1,0:T(8,128)(2,1)}, f32[64,8]{1,0:T(8,128)S(1)}, f32[64,8]{1,0:T(8,128)S(1)}, ...), branch_computations={%region_20.21_spmd, %region_21.22_spmd} | conditional | flops 5398069760 | bytes 208947360 | solution.py:109
  270.0 6.2 %exponential_select_fusion.1 = f32[512,8192]{1,0:T(8,128)S(1)} fusion(bf16[512,128]{1,0:T(8,128)(2,1)S(1)} %get-tuple-element.99, bf16[8192,128]{1,0:T(8,128)(2,1)} %get-tuple-element.100, f32[512]{0:T(512)S(1)} %sub.89, pred[64,8192]{1,0:T(8,128)(4,1)S(1)} %get-tuple-element.98), kind=kOutput, calls=%fused_computation.17 | convolution fusion | flops 1086324736 | bytes 19531776 | tf_op jit(solution)/shard_map/cond/branch_1_fun/dot_general | solution.py:46
  276.2 5.7 %copy-done.1 = f32[512,8192]{1,0:T(8,128)} copy-done((f32[512,8192]{1,0:T(8,128)}, f32[512,8192]{1,0:T(8,128)S(1)}, u32[]{:S(2)}) %copy-start.1) | copy-done | bytes 16777240 | tf_op jit(solution)/shard_map/cond
  286.4 9.4 %multiply_convert_fusion.1 = bf16[512,8192]{1,0:T(8,128)(2,1)} fusion(f32[512,8192]{1,0:T(8,128)} %copy-done.1, bf16[512,128]{1,0:T(8,128)(2,1)S(1)} %get-tuple-element.103, bf16[8192,128]{1,0:T(8,128)(2,1)S(1)} %copy-done.9, f32[512]{0:T(512)S(1)} %sub.92), kind=kOutput, calls=%fused_computation.16 | convolution fusion | flops 1086324736 | bytes 27396096 | tf_op jit(solution)/shard_map/cond/branch_1_fun/dot_general | solution.py:46
  295.8 5.9 %fusion.25 = f32[512,128]{1,0:T(8,128)S(1)} fusion(bf16[512,8192]{1,0:T(8,128)(2,1)} %multiply_convert_fusion.1, bf16[8192,128]{1,0:T(8,128)(2,1)S(1)} %copy-done.5), kind=kOutput, calls=%fused_computation.69 | convolution fusion | flops 1073741824 | bytes 10747904 | tf_op jit(solution)/shard_map/cond/branch_1_fun/dot_general | solution.py:102
  314.0 8.8 %pad_maximum_fusion = f32[8192,2,128]{2,1,0:T(2,128)} fusion(f32[8192,1,128]{2,1,0:T(1,128)S(1)} %bitcast.84, f32[8192,1,128]{2,1,0:T(1,128)S(1)} %bitcast.85), kind=kLoop, calls=%fused_computation.20 | loop fusion | flops 2097152 | bytes 16777216 | tf_op jit(solution)/shard_map/stack | solution.py:165
  324.7 202.1 %all-reduce.3.cloned.1.call-done = f32[8192,2,128]{2,1,0:T(2,128)} async-done(((f32[8192,2,128]{2,1,0:T(2,128)}), f32[8192,2,128]{2,1,0:T(2,128)}) %all-reduce.3.cloned.1.call-update) | async-done | bytes 8388624
  (87 shorter events, 61.3 us)
Async XLA Ops:
  7.2 88.1 %all-gather.3.cloned.1.call-start = ((), (), s32[]{:S(2)}) async-start(), calls=%async_computation.4 | async-start | bytes 2129920 | tf_op jit(solution)/shard_map/all_gather | solution.py:149
  17.6 155.4 %all-gather.5.cloned.1.call-start = ((), (), s32[]{:S(2)}) async-start(), calls=%async_computation.5 | async-start | bytes 2129920 | tf_op jit(solution)/shard_map/all_gather | solution.py:136
  26.9 499.9 %all-reduce.3.cloned.1.call-start = ((), (), s32[]{:S(2)}) async-start(), calls=%async_computation.6 | async-start | bytes 16777216
  173.0 9.6 %copy-start.6 = (bf16[8192,128]{1,0:T(8,128)(2,1)S(1)}, bf16[8192,128]{1,0:T(8,128)(2,1)}, u32[]{:S(2)}) copy-start(bf16[8192,128]{1,0:T(8,128)(2,1)} %get-tuple-element.84) | copy-start | bytes 6291460 | tf_op jit(solution)/shard_map/cond
  173.0 9.6 %copy-start.10 = (bf16[512,128]{1,0:T(8,128)(2,1)S(1)}, bf16[512,128]{1,0:T(8,128)(2,1)}, u32[]{:S(2)}) copy-start(bf16[512,128]{1,0:T(8,128)(2,1)} %get-tuple-element.83) | copy-start | bytes 393220 | tf_op jit(solution)/shard_map/cond
  205.3 11.9 %copy-start.11 = (bf16[512,128]{1,0:T(8,128)(2,1)S(1)}, bf16[512,128]{1,0:T(8,128)(2,1)}, u32[]{:S(2)}) copy-start(bf16[512,128]{1,0:T(8,128)(2,1)} %get-tuple-element.90) | copy-start | bytes 393220 | tf_op jit(solution)/shard_map/cond
  211.5 5.7 %copy-start = (f32[512,8192]{1,0:T(8,128)}, f32[512,8192]{1,0:T(8,128)S(1)}, u32[]{:S(2)}) copy-start(f32[512,8192]{1,0:T(8,128)S(1)} %exponential_select_fusion) | copy-start | bytes 50331652 | tf_op jit(solution)/shard_map/cond
  217.2 4.3 copy-start.7
  221.6 9.4 %copy-start.4 = (bf16[8192,128]{1,0:T(8,128)(2,1)S(1)}, bf16[8192,128]{1,0:T(8,128)(2,1)}, u32[]{:S(2)}) copy-start(bf16[8192,128]{1,0:T(8,128)(2,1)} %get-tuple-element.87) | copy-start | bytes 6291460 | tf_op jit(solution)/shard_map/cond
  231.0 5.9 %copy-start.2 = (bf16[512,8192]{1,0:T(8,128)(2,1)S(1)}, bf16[512,8192]{1,0:T(8,128)(2,1)}, u32[]{:S(2)}) copy-start(bf16[512,8192]{1,0:T(8,128)(2,1)} %multiply_convert_fusion) | copy-start | bytes 25165828 | tf_op jit(solution)/shard_map/cond
  241.4 9.6 %copy-start.8 = (bf16[8192,128]{1,0:T(8,128)(2,1)S(1)}, bf16[8192,128]{1,0:T(8,128)(2,1)}, u32[]{:S(2)}) copy-start(bf16[8192,128]{1,0:T(8,128)(2,1)} %get-tuple-element.97) | copy-start | bytes 6291460 | tf_op jit(solution)/shard_map/cond
  276.2 5.7 %copy-start.1 = (f32[512,8192]{1,0:T(8,128)}, f32[512,8192]{1,0:T(8,128)S(1)}, u32[]{:S(2)}) copy-start(f32[512,8192]{1,0:T(8,128)S(1)} %exponential_select_fusion.1) | copy-start | bytes 50331652 | tf_op jit(solution)/shard_map/cond
  281.9 4.4 copy-start.9
  286.4 9.4 %copy-start.5 = (bf16[8192,128]{1,0:T(8,128)(2,1)S(1)}, bf16[8192,128]{1,0:T(8,128)(2,1)}, u32[]{:S(2)}) copy-start(bf16[8192,128]{1,0:T(8,128)(2,1)} %get-tuple-element.100) | copy-start | bytes 6291460 | tf_op jit(solution)/shard_map/cond
  295.8 5.9 %copy-start.3 = (bf16[512,8192]{1,0:T(8,128)(2,1)S(1)}, bf16[512,8192]{1,0:T(8,128)(2,1)}, u32[]{:S(2)}) copy-start(bf16[512,8192]{1,0:T(8,128)(2,1)} %multiply_convert_fusion.1) | copy-start | bytes 25165828 | tf_op jit(solution)/shard_map/cond
  322.7 0.7 copy-start.12
  529.7 9.7 %all-to-all-start.3 = ((bf16[4,2,2048]{2,1,0:T(2,128)(2,1)}), bf16[4,2,2048]{2,1,0:T(2,128)(2,1)S(1)}, u32[]{:S(2)}, u32[]{:S(2)}) async-start(bf16[4,2,2048]{2,1,0:T(2,128)(2,1)} %reshape.175), calls=%async_computation.3 | async-start | bytes 65536 | tf_op jit(solution)/shard_map/all_to_all | solution.py:177
  539.4 8.7 %all-to-all-start.2 = ((bf16[4,2,2048]{2,1,0:T(2,128)(2,1)}), bf16[4,2,2048]{2,1,0:T(2,128)(2,1)S(1)}, u32[]{:S(2)}, u32[]{:S(2)}) async-start(bf16[4,2,2048]{2,1,0:T(2,128)(2,1)} %reshape.173), calls=%async_computation.2 | async-start | bytes 65536 | tf_op jit(solution)/shard_map/all_to_all | solution.py:176
Sparse Core Ops, SparseCore 0:
  17.8 77.4 all-gather.2
  98.0 74.9 all-gather.4
  322.9 203.8 all-reduce.2
where the time goes:
time: 564 us; the launch traced here: 556 us
  waiting for transfers between devices  347 us (62%)
  matrix products  99.2 us (18%)
  other arithmetic  42 us (7%)
  local copies, waits for them, and re-layouts  24.3 us (4%)
  blocking collectives  18.1 us (3%)
  between operations  16.1 us (3%)
  starting transfers between devices  7.63 us (1%)
    unnamed x4, waiting for transfers between devices  202 us
    all_gather x1, waiting for transfers between devices, body(): lax.all_gather(values, 'ctx', axis=0, tiled=True)  77.8 us
    dot_general x8, matrix products, contract_rows(): lax.dot_general(left, right, (((1,), (1,)), ((), ())), preferred_element_...  70.1 us
    all_gather x1, waiting for transfers between devices, body(): lax.all_gather(keys, 'ctx', axis=0, tiled=True)  60.1 us
    dot_general x4, matrix products, contract_first(): lax.dot_general(left, right, (((0,), (0,)), ((), ())), preferred_element_...  17.4 us
    reduce_sum x2, other arithmetic, stats_compute(): return (new_high, jnp.sum(probs, axis=2), jnp.sum(probs * d_probs, axis=2))  17 us
    dot_general x2, matrix products, grad_compute(): grad_rows = jnp.dot(d_scores, keys, preferred_element_type=jnp.float32)  11.7 us
    cond x24, local copies, waits for them, and re-layouts  11.4 us
  transfers between devices with their start and end apart: 5, of which 5 were waited for; matrix products, arithmetic and copies ran while one was open for 2% of the time, Pallas kernels for 0%

commit v1 on v0

--- a/solution.py
+++ b/solution.py
@@ -133,7 +133,9 @@
     )
     piece = (
         lax.all_gather(keys, "ctx", axis=0, tiled=True),
-        lax.all_gather(values, "ctx", axis=0, tiled=True),
+        jnp.concatenate(
+            lax.all_to_all(jnp.stack(lax.axis_size("ctx") * [values]), "ctx", 0, 0), axis=0
+        ),
     )
     stats = tuple(
         (

time: 564 us -> 539 us (0.956)
  waiting for transfers between devices: 347 us -> 311 us
  starting transfers between devices: 7.63 us -> 19.9 us
    all_gather x1, waiting for transfers between devices: 77.8 us -> 49.6 us  [body(): lax.all_gather(values, 'ctx', axis=0, tiled=True)]
    all_to_all x0 -> x1, starting transfers between devices: none -> 12.3 us  [body(): lax.all_to_all(jnp.stack(lax.axis_size('ctx') * [values]), 'ctx', 0, 0)]
    all_gather x1, waiting for transfers between devices: 60.1 us -> 51.5 us  [body(): lax.all_gather(keys, 'ctx', axis=0, tiled=True)]
    cond x24 -> x18, local copies, waits for them, and re-layouts: 11.4 us -> 11.4 us
  transfers between devices with their start and end apart: 5 -> 6, of which waited for: 5 -> 5; matrix products, arithmetic and copies ran while one was open for 2% -> 8% of each run, Pallas kernels for 0% -> 0%
where the time goes in v1:
time: 539 us; the launch traced here: 530 us
  waiting for transfers between devices  311 us (58%)
  matrix products  100 us (19%)
  other arithmetic  41.3 us (8%)
  local copies, waits for them, and re-layouts  22.8 us (4%)
  starting transfers between devices  19.9 us (4%)
  blocking collectives  17.4 us (3%)
  between operations  16.1 us (3%)
    unnamed x4, waiting for transfers between devices  203 us
    dot_general x8, matrix products, contract_rows(): lax.dot_general(left, right, (((1,), (1,)), ((), ())), preferred_element_...  71.1 us
    all_gather x1, waiting for transfers between devices, body(): lax.all_gather(keys, 'ctx', axis=0, tiled=True)  51.5 us
    all_gather x1, waiting for transfers between devices, body(): lax.all_gather(values, 'ctx', axis=0, tiled=True)  49.6 us
    dot_general x4, matrix products, contract_first(): lax.dot_general(left, right, (((0,), (0,)), ((), ())), preferred_element_...  17.4 us
    reduce_sum x2, other arithmetic, stats_compute(): return (new_high, jnp.sum(probs, axis=2), jnp.sum(probs * d_probs, axis=2))  17 us
    all_to_all x1, starting transfers between devices, body(): lax.all_to_all(jnp.stack(lax.axis_size('ctx') * [values]), 'ctx', 0, 0)  12.3 us
    dot_general x2, matrix products, grad_compute(): grad_rows = jnp.dot(d_scores, keys, preferred_element_type=jnp.float32)  11.7 us
  transfers between devices with their start and end apart: 6, of which 5 were waited for; matrix products, arithmetic and copies ran while one was open for 8% of the time, Pallas kernels for 0%

profile of v1, /device:TPU:8, one launch (start us, length us, event | category | flops | bytes accessed | tf_op | source)
XLA Modules:
  0.0 530.1 jit_solution(4763304610498905523)
XLA Ops:
  8.0 9.6 %all_to_all.71 = bf16[32,4,128]{2,0,1:T(8,128)(2,1)} all-to-all(bf16[32,4,128]{2,0,1:T(8,128)(2,1)S(1)} %copy.34), channel_id=1, replica_groups=mesh['ctx'=64,'head'=4] {'head'}, dimensions={1} | all-to-all | bytes 65536 | tf_op jit(solution)/shard_map/all_to_all | solution.py:114
  18.4 7.8 %all_to_all.72 = bf16[32,4,128]{2,0,1:T(8,128)(2,1)S(1)} all-to-all(bf16[32,4,128]{2,0,1:T(8,128)(2,1)S(1)} %copy.35), channel_id=1, replica_groups=mesh['ctx'=64,'head'=4] {'head'}, dimensions={1} | all-to-all | bytes 65536 | tf_op jit(solution)/shard_map/all_to_all | solution.py:115
  28.0 12.3 %all-to-all-start.2 = ((bf16[64,128,128]{2,1,0:T(8,128)(2,1)}), bf16[64,128,128]{2,1,0:T(8,128)(2,1)}, u32[]{:S(2)}, u32[]{:S(2)}) async-start(bf16[64,128,128]{2,1,0:T(8,128)(2,1)} %stack.12), calls=%async_computation.2 | async-start | bytes 4194304 | tf_op jit(solution)/shard_map/all_to_all | solution.py:137
  48.6 51.5 %all-gather.3.cloned.1.call-done = bf16[8192,128]{1,0:T(8,128)(2,1)} async-done(((bf16[128,128]{1,0:T(8,128)(2,1)}), bf16[8192,128]{1,0:T(8,128)(2,1)}) %all-gather.3.cloned.1.call-update) | async-done | bytes 2097168 | tf_op jit(solution)/shard_map/all_gather | solution.py:151
  100.2 28.6 %conditional.6 = (f32[64,8]{1,0:T(8,128)S(1)}, f32[64,8]{1,0:T(8,128)S(1)}, f32[64,8]{1,0:T(8,128)S(1)}) conditional(s32[]{:T(128)} %convert_element_type.38, () %tuple.61, (pred[64,8192]{1,0:T(8,128)(4,1)S(1)}, bf16[512,128]{1,0:T(8,128)(2,1)S(1)}, bf16[8192,128]{1,0:T(8,128)(2,1)}, bf16[512,128]{1,0:T(8,128)(2,1)S(1)}, ...), branch_computations={%region_15.16_spmd, %region_16.20_spmd} | conditional | flops 2197814784 | bytes 56395800 | solution.py:77
  100.2 9.4 %fusion.4 = (f32[512]{0:T(512)S(1)}, f32[512,8192]{1,0:T(8,128)}) fusion(pred[64,8192]{1,0:T(8,128)(4,1)S(1)} %get-tuple-element.93, bf16[512,128]{1,0:T(8,128)(2,1)S(1)} %get-tuple-element.94, bf16[8192,128]{1,0:T(8,128)(2,1)} %get-tuple-element.95), kind=kOutput, calls=%fused_computation.12 | convolution fusion | flops 1086324224 | bytes 19531776 | tf_op jit(solution)/shard_map/cond/branch_1_fun/dot_general | solution.py:46
  109.6 10.5 %multiply_reduce_fusion.1 = f32[512]{0:T(512)S(1)} fusion(bf16[512,128]{1,0:T(8,128)(2,1)S(1)} %get-tuple-element.96, bf16[8192,128]{1,0:T(8,128)(2,1)} %get-tuple-element.97, f32[512,8192]{1,0:T(8,128)} %get-tuple-element.176, f32[512]{0:T(512)S(1)} %broadcast_maximum_fusion.1, pred[64,8192]{1,0:T(8,128)(4,1)S(1)} %get-tuple-element.93), kind=kOutput, calls=%fused_computation.13 | convolution fusion | flops 1094712832 | bytes 19533824 | tf_op jit(solution)/shard_map/cond/branch_1_fun/dot_general | solution.py:46
  120.0 8.5 %fusion.5 = f32[512]{0:T(512)S(1)} fusion(f32[512,8192]{1,0:T(8,128)} %get-tuple-element.176, f32[512]{0:T(512)S(1)} %broadcast_maximum_fusion.1, pred[64,8192]{1,0:T(8,128)(4,1)S(1)} %get-tuple-element.93), kind=kLoop, calls=%fused_computation.14 | loop fusion | flops 16776704 | bytes 17305600 | tf_op jit(solution)/shard_map/cond/branch_1_fun/reduce_sum | solution.py:72
  128.8 49.6 %all-gather.5.cloned.1.call-done = bf16[8192,128]{1,0:T(8,128)(2,1)} async-done(((bf16[128,128]{1,0:T(8,128)(2,1)}), bf16[8192,128]{1,0:T(8,128)(2,1)}) %all-gather.5.cloned.1.call-update) | async-done | bytes 2097168 | tf_op jit(solution)/shard_map/all_gather | solution.py:152
  178.4 36.9 %conditional.7 = (f32[512,128]{1,0:T(8,128)S(1)}, f32[8192,128]{1,0:T(8,128)}, f32[8192,128]{1,0:T(8,128)}) conditional(s32[]{:T(128)} %convert_element_type.38, () %tuple.60, (pred[64,8192]{1,0:T(8,128)(4,1)S(1)}, bf16[512,128]{1,0:T(8,128)(2,1)S(1)}, bf16[8192,128]{1,0:T(8,128)(2,1)}, f32[64,8]{1,0:T(8,128)S(1)}, f32[64,8]{1,0:T(8,128)S(1)}, ...), branch_computations={%region_20.21_spmd, %region_21.22_spmd} | conditional | flops 5398069760 | bytes 209471680 | solution.py:109
  179.2 6.2 %exponential_select_fusion.1 = f32[512,8192]{1,0:T(8,128)S(1)} fusion(bf16[512,128]{1,0:T(8,128)(2,1)S(1)} %get-tuple-element.99, bf16[8192,128]{1,0:T(8,128)(2,1)} %get-tuple-element.100, f32[512]{0:T(512)S(1)} %sub.89, pred[64,8192]{1,0:T(8,128)(4,1)S(1)} %get-tuple-element.98), kind=kOutput, calls=%fused_computation.17 | convolution fusion | flops 1086324736 | bytes 19531776 | tf_op jit(solution)/shard_map/cond/branch_1_fun/dot_general | solution.py:46
  185.4 5.7 %copy-done = f32[512,8192]{1,0:T(8,128)} copy-done((f32[512,8192]{1,0:T(8,128)}, f32[512,8192]{1,0:T(8,128)S(1)}, u32[]{:S(2)}) %copy-start) | copy-done | bytes 16777240 | tf_op jit(solution)/shard_map/cond
  195.5 9.6 %multiply_convert_fusion.1 = bf16[512,8192]{1,0:T(8,128)(2,1)} fusion(f32[512,8192]{1,0:T(8,128)} %copy-done, bf16[512,128]{1,0:T(8,128)(2,1)} %copy-done.8, bf16[8192,128]{1,0:T(8,128)(2,1)S(1)} %copy-done.6, f32[512]{0:T(512)S(1)} %sub.92), kind=kOutput, calls=%fused_computation.16 | convolution fusion | flops 1086324736 | bytes 27396096 | tf_op jit(solution)/shard_map/cond/branch_1_fun/dot_general | solution.py:46
  205.1 5.9 %fusion.25 = f32[512,128]{1,0:T(8,128)S(1)} fusion(bf16[512,8192]{1,0:T(8,128)(2,1)} %multiply_convert_fusion.1, bf16[8192,128]{1,0:T(8,128)(2,1)S(1)} %copy-done.4), kind=kOutput, calls=%fused_computation.69 | convolution fusion | flops 1073741824 | bytes 10747904 | tf_op jit(solution)/shard_map/cond/branch_1_fun/dot_general | solution.py:102
  215.3 28.8 %conditional.4 = (f32[64,8]{1,0:T(8,128)S(1)}, f32[64,8]{1,0:T(8,128)S(1)}, f32[64,8]{1,0:T(8,128)S(1)}) conditional(s32[]{:T(128)} %convert_element_type.36, () %tuple.57, (pred[64,8192]{1,0:T(8,128)(4,1)S(1)}, bf16[512,128]{1,0:T(8,128)(2,1)S(1)}, bf16[8192,128]{1,0:T(8,128)(2,1)}, bf16[512,128]{1,0:T(8,128)(2,1)S(1)}, ...), branch_computations={%region_5.6_spmd, %region_6.10_spmd} | conditional | flops 2197814784 | bytes 56395800 | solution.py:77
  215.5 9.4 %fusion = (f32[512]{0:T(512)S(1)}, f32[512,8192]{1,0:T(8,128)}) fusion(pred[64,8192]{1,0:T(8,128)(4,1)S(1)} %get-tuple-element.80, bf16[512,128]{1,0:T(8,128)(2,1)S(1)} %get-tuple-element.81, bf16[8192,128]{1,0:T(8,128)(2,1)} %get-tuple-element.82), kind=kOutput, calls=%fused_computation.2 | convolution fusion | flops 1086324224 | bytes 19531776 | tf_op jit(solution)/shard_map/cond/branch_1_fun/dot_general | solution.py:46
  224.9 10.5 %multiply_reduce_fusion = f32[512]{0:T(512)S(1)} fusion(bf16[512,128]{1,0:T(8,128)(2,1)S(1)} %get-tuple-element.83, bf16[8192,128]{1,0:T(8,128)(2,1)} %get-tuple-element.84, f32[512,8192]{1,0:T(8,128)} %get-tuple-element.172, f32[512]{0:T(512)S(1)} %broadcast_maximum_fusion, pred[64,8192]{1,0:T(8,128)(4,1)S(1)} %get-tuple-element.80), kind=kOutput, calls=%fused_computation.3 | convolution fusion | flops 1094712832 | bytes 19533824 | tf_op jit(solution)/shard_map/cond/branch_1_fun/dot_general | solution.py:46
  235.4 8.5 %fusion.1 = f32[512]{0:T(512)S(1)} fusion(f32[512,8192]{1,0:T(8,128)} %get-tuple-element.172, f32[512]{0:T(512)S(1)} %broadcast_maximum_fusion, pred[64,8192]{1,0:T(8,128)(4,1)S(1)} %get-tuple-element.80), kind=kLoop, calls=%fused_computation.4 | loop fusion | flops 16776704 | bytes 17305600 | tf_op jit(solution)/shard_map/cond/branch_1_fun/reduce_sum | solution.py:72
  244.1 36.5 %conditional.5 = (f32[512,128]{1,0:T(8,128)S(1)}, f32[8192,128]{1,0:T(8,128)}, f32[8192,128]{1,0:T(8,128)}) conditional(s32[]{:T(128)} %convert_element_type.36, () %tuple.56, (pred[64,8192]{1,0:T(8,128)(4,1)S(1)}, bf16[512,128]{1,0:T(8,128)(2,1)S(1)}, bf16[8192,128]{1,0:T(8,128)(2,1)}, f32[64,8]{1,0:T(8,128)S(1)}, f32[64,8]{1,0:T(8,128)S(1)}, ...), branch_computations={%region_10.11_spmd, %region_11.12_spmd} | conditional | flops 5398069760 | bytes 208947360 | solution.py:109
  244.6 6.2 %exponential_select_fusion = f32[512,8192]{1,0:T(8,128)S(1)} fusion(bf16[512,128]{1,0:T(8,128)(2,1)S(1)} %get-tuple-element.86, bf16[8192,128]{1,0:T(8,128)(2,1)} %get-tuple-element.87, f32[512]{0:T(512)S(1)} %sub.81, pred[64,8192]{1,0:T(8,128)(4,1)S(1)} %get-tuple-element.85), kind=kOutput, calls=%fused_computation.7 | convolution fusion | flops 1086324736 | bytes 19531776 | tf_op jit(solution)/shard_map/cond/branch_1_fun/dot_general | solution.py:46
  260.8 9.4 %multiply_convert_fusion = bf16[512,8192]{1,0:T(8,128)(2,1)} fusion(f32[512,8192]{1,0:T(8,128)} %copy-done.1, bf16[512,128]{1,0:T(8,128)(2,1)S(1)} %get-tuple-element.90, bf16[8192,128]{1,0:T(8,128)(2,1)S(1)} %copy-done.7, f32[512]{0:T(512)S(1)} %sub.84), kind=kOutput, calls=%fused_computation.6 | convolution fusion | flops 1086324736 | bytes 27396096 | tf_op jit(solution)/shard_map/cond/branch_1_fun/dot_general | solution.py:46
  270.3 5.9 %fusion.23 = f32[512,128]{1,0:T(8,128)S(1)} fusion(bf16[512,8192]{1,0:T(8,128)(2,1)} %multiply_convert_fusion, bf16[8192,128]{1,0:T(8,128)(2,1)S(1)} %copy-done.5), kind=kOutput, calls=%fused_computation.67 | convolution fusion | flops 1073741824 | bytes 10747904 | tf_op jit(solution)/shard_map/cond/branch_1_fun/dot_general | solution.py:102
  288.5 8.8 %pad_maximum_fusion = f32[8192,2,128]{2,1,0:T(2,128)} fusion(f32[8192,1,128]{2,1,0:T(1,128)S(1)} %bitcast.85, f32[8192,1,128]{2,1,0:T(1,128)S(1)} %bitcast.86), kind=kLoop, calls=%fused_computation.20 | loop fusion | flops 2097152 | bytes 16777216 | tf_op jit(solution)/shard_map/stack | solution.py:167
  299.2 202.1 %all-reduce.3.cloned.1.call-done = f32[8192,2,128]{2,1,0:T(2,128)} async-done(((f32[8192,2,128]{2,1,0:T(2,128)}), f32[8192,2,128]{2,1,0:T(2,128)}) %all-reduce.3.cloned.1.call-update) | async-done | bytes 8388624
  (86 shorter events, 65.5 us)
Async XLA Ops:
  7.2 93.0 %all-gather.3.cloned.1.call-start = ((), (), s32[]{:S(2)}) async-start(), calls=%async_computation.5 | async-start | bytes 2129920 | tf_op jit(solution)/shard_map/all_gather | solution.py:151
  26.2 14.2 %copy-start.9 = (bf16[32,4,128]{2,0,1:T(8,128)(2,1)}, bf16[32,4,128]{2,0,1:T(8,128)(2,1)S(1)}, u32[]{:S(2)}) copy-start(bf16[32,4,128]{2,0,1:T(8,128)(2,1)S(1)} %all_to_all.72) | copy-start | bytes 98308
  28.0 72.2 %all-to-all-start.2 = ((bf16[64,128,128]{2,1,0:T(8,128)(2,1)}), bf16[64,128,128]{2,1,0:T(8,128)(2,1)}, u32[]{:S(2)}, u32[]{:S(2)}) async-start(bf16[64,128,128]{2,1,0:T(8,128)(2,1)} %stack.12), calls=%async_computation.2 | async-start | bytes 4194304 | tf_op jit(solution)/shard_map/all_to_all | solution.py:137
  40.3 138.1 %all-gather.5.cloned.1.call-start = ((), (), s32[]{:S(2)}) async-start(), calls=%async_computation.6 | async-start | bytes 2129920 | tf_op jit(solution)/shard_map/all_gather | solution.py:152
  41.1 460.3 %all-reduce.3.cloned.1.call-start = ((), (), s32[]{:S(2)}) async-start(), calls=%async_computation.7 | async-start | bytes 16777216
  179.0 6.4 %copy-start.8 = (bf16[512,128]{1,0:T(8,128)(2,1)}, bf16[512,128]{1,0:T(8,128)(2,1)S(1)}, u32[]{:S(2)}) copy-start(bf16[512,128]{1,0:T(8,128)(2,1)S(1)} %get-tuple-element.103) | copy-start | bytes 393220 | tf_op jit(solution)/shard_map/cond
  185.3 5.7 %copy-start = (f32[512,8192]{1,0:T(8,128)}, f32[512,8192]{1,0:T(8,128)S(1)}, u32[]{:S(2)}) copy-start(f32[512,8192]{1,0:T(8,128)S(1)} %exponential_select_fusion.1) | copy-start | bytes 50331652 | tf_op jit(solution)/shard_map/cond
  191.1 4.4 copy-start.6
  195.5 9.6 %copy-start.4 = (bf16[8192,128]{1,0:T(8,128)(2,1)S(1)}, bf16[8192,128]{1,0:T(8,128)(2,1)}, u32[]{:S(2)}) copy-start(bf16[8192,128]{1,0:T(8,128)(2,1)} %get-tuple-element.100) | copy-start | bytes 6291460 | tf_op jit(solution)/shard_map/cond
  205.1 5.9 %copy-start.2 = (bf16[512,8192]{1,0:T(8,128)(2,1)S(1)}, bf16[512,8192]{1,0:T(8,128)(2,1)}, u32[]{:S(2)}) copy-start(bf16[512,8192]{1,0:T(8,128)(2,1)} %multiply_convert_fusion.1) | copy-start | bytes 25165828 | tf_op jit(solution)/shard_map/cond
  250.7 5.7 %copy-start.1 = (f32[512,8192]{1,0:T(8,128)}, f32[512,8192]{1,0:T(8,128)S(1)}, u32[]{:S(2)}) copy-start(f32[512,8192]{1,0:T(8,128)S(1)} %exponential_select_fusion) | copy-start | bytes 50331652 | tf_op jit(solution)/shard_map/cond
  256.5 4.4 copy-start.7
  260.8 9.4 %copy-start.5 = (bf16[8192,128]{1,0:T(8,128)(2,1)S(1)}, bf16[8192,128]{1,0:T(8,128)(2,1)}, u32[]{:S(2)}) copy-start(bf16[8192,128]{1,0:T(8,128)(2,1)} %get-tuple-element.87) | copy-start | bytes 6291460 | tf_op jit(solution)/shard_map/cond
  270.3 5.9 %copy-start.3 = (bf16[512,8192]{1,0:T(8,128)(2,1)S(1)}, bf16[512,8192]{1,0:T(8,128)(2,1)}, u32[]{:S(2)}) copy-start(bf16[512,8192]{1,0:T(8,128)(2,1)} %multiply_convert_fusion) | copy-start | bytes 25165828 | tf_op jit(solution)/shard_map/cond
  297.2 0.7 copy-start.10
  504.3 9.7 %all-to-all-start.4 = ((bf16[4,2,2048]{2,1,0:T(2,128)(2,1)}), bf16[4,2,2048]{2,1,0:T(2,128)(2,1)S(1)}, u32[]{:S(2)}, u32[]{:S(2)}) async-start(bf16[4,2,2048]{2,1,0:T(2,128)(2,1)} %reshape.182), calls=%async_computation.4 | async-start | bytes 65536 | tf_op jit(solution)/shard_map/all_to_all | solution.py:179
  514.0 8.7 %all-to-all-start.3 = ((bf16[4,2,2048]{2,1,0:T(2,128)(2,1)}), bf16[4,2,2048]{2,1,0:T(2,128)(2,1)S(1)}, u32[]{:S(2)}, u32[]{:S(2)}) async-start(bf16[4,2,2048]{2,1,0:T(2,128)(2,1)} %reshape.180), calls=%async_computation.3 | async-start | bytes 65536 | tf_op jit(solution)/shard_map/all_to_all | solution.py:178
Sparse Core Ops, SparseCore 0:
  17.8 82.3 all-gather.2
  103.5 74.8 all-gather.4
  297.4 203.8 all-reduce.2
